TPU v7x, 32 devices: a whole 2x2x4 slice. The times are simulated.
32 devices in a mesh: groups: 2 (over x), view: 16 (over z, y, core).
Axes of the slice: x: 2, y: 2, z: 4, core: 2. Of those that a mesh axis runs over, the one named last changes fastest.
Arguments:
- ref_features: bfloat16 [256, 32, 384], P(('groups', 'view')), parts along dimension 0, may hold values from -6 to 6
- source_tiles: bfloat16 [1024, 2, 32, 384], P(('groups', 'view')), parts along dimension 0, may hold values from -6 to 6
- pair_lists: int32 [32, 4, 4], P(('groups', 'view')), parts along dimension 0, may hold values from -1 to 511, as said below
- view_counts: int32 [32], P(('groups', 'view')), parts along dimension 0, may hold values from 3 to 4, as said below
- disparities: int32 [16, 4], P('groups'), parts along dimension 0, may hold values from -48 to 48
- conv_first: bfloat16 [3, 3, 8, 3, 32], replicated, may hold values from -0.21875 to 0.21875
- bias_first: float32 [8], replicated, may hold values from -3 to 3
- conv_second: bfloat16 [16, 3, 3, 3, 8], replicated, may hold values from -0.4375 to 0.4375
- bias_second: float32 [16], replicated, may hold values from -3 to 3
Outputs:
- cost_features: float32 [8, 64, 16, 192], P('groups', 'view'), parts along dimension 0
There are 2 independent parts, one for each index of `groups`. A program takes and returns all parts, laid end to end along the dimension named above; an argument that names none is the same for every part. Nothing has to cross between parts.
Inputs may be any that keep to these rules, and one draw needn't show every extreme that they name: pair_lists[v, s, b] is the tile holding rows 2b and 2b + 1 of source s of strip v; it is -1 exactly when s >= view_counts[v]; tile t lies on device t // 32 of the view axis; no strip takes more than 2 tiles from one device, and some strip takes exactly 2 from some device. `view_counts`: some strip uses 3 sources and some uses 4.
All inputs are finite; a program needn't handle non-finite values.
Results may differ from a plain program's by a relative error of at most 0.0028.
Values may be sent and summed in bfloat16 or wider, within the bound.
A program may use at most 128 MiB of HBM per device.

v0:
```python
import functools

import jax
import jax.numpy as jnp
from jax import lax
from jax.experimental import pallas as pl
from jax.experimental.pallas import tpu as pltpu
from jax.sharding import PartitionSpec as P


def passed_along(x, axis, by):
    count = lax.axis_size(axis)
    pairs = [(i, i + by) for i in range(count) if 0 <= i + by < count]
    return lax.ppermute(x, axis, pairs)


def request_slots(flat_ids, slot_cap, tiles_dev):
    is_live = flat_ids >= 0
    owners = jnp.where(is_live, flat_ids // tiles_dev, -1)
    count_req = flat_ids.shape[0]
    earlier = jnp.arange(count_req)[None, :] < jnp.arange(count_req)[:, None]
    same_owner = (owners[:, None] == owners[None, :]) & earlier & is_live[None, :]
    slot_rank = jnp.sum(same_owner.astype(jnp.int32), axis=1)
    slot_ids = jnp.where(is_live, owners * slot_cap + slot_rank, -1)
    return (slot_ids, flat_ids % tiles_dev)


def request_table(slot_ids, local_ids, n_view, slot_cap):
    positions = jnp.arange(n_view * slot_cap)
    matches = slot_ids[:, None] == positions[None, :]
    wanted = jnp.sum(jnp.where(matches, local_ids[:, None] + 1, 0), axis=0) - 1
    return wanted.reshape(n_view, slot_cap)


def ask_kernel(n_view, wanted_ref, asked_ref, send_sem, recv_sem):
    me = lax.axis_index("view")
    mesh_id = pl.DeviceIdType.MESH
    barrier = pltpu.get_barrier_semaphore()

    def greet(step, carry):
        peer = lax.rem(me + step, n_view)
        pl.semaphore_signal(barrier, inc=1, device_id={"view": peer}, device_id_type=mesh_id)
        return carry

    lax.fori_loop(1, n_view, greet, 0)
    pl.semaphore_wait(barrier, n_view - 1)

    def ask(step, carry):
        peer = lax.rem(me + step, n_view)
        pltpu.make_async_remote_copy(
            src_ref=wanted_ref.at[peer],
            dst_ref=asked_ref.at[me],
            send_sem=send_sem.at[peer],
            recv_sem=recv_sem.at[me],
            device_id={"view": peer},
            device_id_type=mesh_id,
        ).start()
        return carry

    lax.fori_loop(1, n_view, ask, 0)
    asked_ref[me] = wanted_ref[me]

    def settle(step, carry):
        peer = lax.rem(me + step, n_view)
        copy = pltpu.make_async_remote_copy(
            src_ref=wanted_ref.at[peer],
            dst_ref=asked_ref.at[peer],
            send_sem=send_sem.at[peer],
            recv_sem=recv_sem.at[peer],
            device_id={"view": peer},
            device_id_type=mesh_id,
        )
        copy.wait_send()
        copy.wait_recv()
        return carry

    lax.fori_loop(1, n_view, settle, 0)


def ask_owners(wanted):
    n_view, slot_cap = wanted.shape
    table = jnp.broadcast_to(
        jnp.pad(wanted, ((0, 0), (0, 128 - slot_cap)))[:, None, :], (n_view, 8, 128)
    )
    vmem = pl.BlockSpec(memory_space=pltpu.VMEM)
    asked = pl.pallas_call(
        functools.partial(ask_kernel, n_view),
        out_shape=jax.ShapeDtypeStruct(table.shape, jnp.int32),
        in_specs=[vmem],
        out_specs=vmem,
        scratch_shapes=[pltpu.SemaphoreType.DMA((n_view,)), pltpu.SemaphoreType.DMA((n_view,))],
        compiler_params=pltpu.CompilerParams(
            collective_id=0, has_side_effects=True, vmem_limit_bytes=4 << 20
        ),
        name="ask",
    )(table)
    return asked[:, 0, :slot_cap]


def variance_kernel(rows, slot_ref, disp_ref, count_ref, arrived_ref, ref_ref, *refs):
    out_refs, wide_ref = refs[:-1], refs[-1]
    sources = slot_ref.shape[0]
    planes = disp_ref.shape[0]
    tile_rows, n_cols = arrived_ref.shape[1:]
    chunk = tile_rows // 2
    live = count_ref[0]
    flat_rows = [row for group in rows for row in group]
    for source in range(sources):
        for place, row in enumerate(flat_rows):
            slot = jnp.maximum(slot_ref[source, row // 2], 0)
            start = (row % 2) * chunk
            tile = arrived_ref[slot, start : start + chunk].astype(jnp.float32)
            wide_ref[source, place] = jnp.where(source < live, tile, 0.0)
    total = live.astype(jnp.float32) + 1.0
    inverse = 1.0 / jnp.full((1, n_cols), total, jnp.float32)
    column = lax.broadcasted_iota(jnp.int32, (chunk, n_cols), 1)

    def one_plane(plane, carry):
        offsets = [disp_ref[plane, source] for source in range(sources)]
        place = 0
        for group, out_ref in zip(rows, out_refs):
            for at, row in enumerate(group):
                summed = ref_ref[row * chunk : (row + 1) * chunk].astype(jnp.float32)
                squares = summed * summed
                for source in range(sources):
                    offset = offsets[source]
                    turned = pltpu.roll(
                        wide_ref[source, place], jnp.where(offset < 0, offset + n_cols, offset), 1
                    )
                    origin = column - offset
                    inside = (origin >= 0) & (origin < n_cols)
                    turned = jnp.where(inside, turned, 0.0)
                    summed = summed + turned
                    squares = squares + turned * turned
                mean = summed * inverse
                out_ref[plane, at * chunk : (at + 1) * chunk] = (
                    squares * inverse - mean * mean
                ).astype(jnp.bfloat16)
                place += 1
        return carry

    lax.fori_loop(0, planes, one_plane, 0)


def variance(rows, slots, disparities, view_counts, arrived, ref_flat):
    planes = disparities.shape[0]
    sources = slots.shape[0]
    chunk, n_cols = (arrived.shape[1] // 2, arrived.shape[2])
    smem = pl.BlockSpec(memory_space=pltpu.SMEM)
    vmem = pl.BlockSpec(memory_space=pltpu.VMEM)
    count = sum(len(group) for group in rows)
    values = planes * count * chunk * n_cols
    return pl.pallas_call(
        functools.partial(variance_kernel, rows),
        out_shape=[
            jax.ShapeDtypeStruct((planes, len(group) * chunk, n_cols), jnp.bfloat16)
            for group in rows
        ],
        in_specs=[smem, smem, smem, vmem, vmem],
        out_specs=[vmem] * len(rows),
        scratch_shapes=[pltpu.VMEM((sources, count, chunk, n_cols), jnp.float32)],
        cost_estimate=pl.CostEstimate(
            flops=values * 40, bytes_accessed=values * 4, transcendentals=0
        ),
        compiler_params=pltpu.CompilerParams(vmem_limit_bytes=12 << 20),
        name="variance%d" % count,
    )(slots, disparities, view_counts, arrived, ref_flat)


def prepare_kernel(conv_ref, w1_ref, pick_ref):
    groups, c1, n_lanes = conv_ref.shape
    rows_out = w1_ref.shape[0] // (groups * c1)
    width = w1_ref.shape[1]
    channels = width // (rows_out + 2)
    bands = []
    for group in range(groups):
        base = conv_ref[group].astype(jnp.float32)
        for hi in range(rows_out):
            bands.append(pltpu.roll(base, hi * channels, 1) if hi else base)
    w1_ref[...] = jnp.concatenate(bands, axis=0).astype(jnp.bfloat16)[:, :width]
    n_cols = pick_ref.shape[0]
    wide = pick_ref.shape[1] // 3
    source = lax.broadcasted_iota(jnp.int32, (n_cols, wide), 0)
    target = lax.broadcasted_iota(jnp.int32, (n_cols, wide), 1)
    for tap in range(3):
        hit = (source == 2 * target + (tap - 1)) & (target < n_cols // 2)
        pick_ref[:, tap * wide : (tap + 1) * wide] = jnp.where(hit, 1.0, 0.0).astype(jnp.bfloat16)


def conv_kernel(
    first_strip_ref, above_ref, top_ref, mid_ref, low_ref, below_ref, w1_ref, b1_ref, w2_ref, b2_ref, pick_ref,
    out_ref, acc_ref, cost_ref,
):
    planes, _, n_cols = mid_ref.shape
    half = w1_ref.shape[0] // 9
    part = 2 * half
    depth = w1_ref.shape[1]
    half_p, half_r, c2, half_x = out_ref.shape
    wide = pick_ref.shape[1] // 3
    weights = w1_ref[...]

    def one_plane(plane):
        strips = (above_ref, top_ref, mid_ref, low_ref, below_ref)
        block = jnp.concatenate([strip[plane] for strip in strips], axis=0)
        skip = depth // (half_r + 3) * (half_r + 1)
        lower = block[skip:]
        products = (
            jnp.dot(weights, block[:depth], preferred_element_type=jnp.float32),
            jnp.dot(weights[:, : lower.shape[0]], lower, preferred_element_type=jnp.float32),
        )
        for tap in range(3):
            target = plane + 1 - tap
            if 0 <= target < planes:
                for shift in range(3):
                    for side in range(2):
                        start = (tap * 3 + shift) * half
                        piece = products[side][start : start + half]
                        at = slice(shift * part + side * half, shift * part + (side + 1) * half)
                        if tap == 0 or (tap == 1 and plane == 0):
                            acc_ref[target, at] = piece
                        else:
                            acc_ref[target, at] += piece

    column = lax.broadcasted_iota(jnp.int32, (part, n_cols), 1)
    row = lax.broadcasted_iota(jnp.int32, (part, n_cols), 0)
    hidden = (row < part // (2 * half_r + 2)) & (first_strip_ref[0] == 1)
    cost_ref[0] = jnp.zeros(cost_ref.shape[1:], cost_ref.dtype)

    def finish(plane):
        left = jnp.where(column == 0, 0.0, pltpu.roll(acc_ref[plane, 0:part], 1, 1))
        right = jnp.where(
            column == n_cols - 1, 0.0, pltpu.roll(acc_ref[plane, 2 * part : 3 * part], n_cols - 1, 1)
        )
        total = acc_ref[plane, part : 2 * part] + left + right + b1_ref[...]
        cost = jnp.where(hidden, 0.0, jnp.maximum(total, 0.0)).astype(jnp.bfloat16)
        spread = jnp.dot(cost, pick_ref[...], preferred_element_type=jnp.float32)
        spread = spread.astype(jnp.bfloat16)
        for tap in range(3):
            cost_ref[plane + 1, tap * part : (tap + 1) * part] = spread[
                :, tap * wide : (tap + 1) * wide
            ]

    def second(q):
        block = cost_ref[2 * q : 2 * q + 3].reshape(9 * part, wide)
        result = jnp.dot(w2_ref[...], block, preferred_element_type=jnp.float32)
        result = result + b2_ref[...]
        out_ref[q] = result[:, :half_x].reshape(half_r, c2, half_x)

    for plane in range(planes):
        one_plane(plane)
        if plane >= 1:
            finish(plane - 1)
            if plane % 2 == 0:
                second(plane // 2 - 1)
    finish(planes - 1)
    second(half_p - 1)


def prepare(conv_first, rows_n, n_cols, wide):
    taps_p, taps_r, c1, taps_x, channels = conv_first.shape
    half_rows = (rows_n + 2) // 2
    width = (half_rows + 2) * channels
    lanes = -(-width // 128) * 128
    groups = taps_p * taps_x
    moved = jnp.transpose(conv_first, (0, 3, 2, 1, 4)).reshape(groups, c1, taps_r * channels)
    moved = jnp.pad(moved, ((0, 0), (0, 0), (0, lanes - taps_r * channels)))
    vmem = pl.BlockSpec(memory_space=pltpu.VMEM)
    return pl.pallas_call(
        prepare_kernel,
        out_shape=[
            jax.ShapeDtypeStruct((groups * half_rows * c1, width), jnp.bfloat16),
            jax.ShapeDtypeStruct((n_cols, 3 * wide), jnp.bfloat16),
        ],
        in_specs=[vmem],
        out_specs=[vmem] * 2,
        cost_estimate=pl.CostEstimate(flops=2000000, bytes_accessed=1200000, transcendentals=0),
        compiler_params=pltpu.CompilerParams(vmem_limit_bytes=8 << 20),
        name="prepare",
    )(moved)


def banded_second(conv_second, rows_n):
    c2, taps_p, taps_r, taps_x, c1 = conv_second.shape
    moved = jnp.transpose(conv_second, (0, 1, 3, 2, 4))
    bands = [
        jnp.pad(
            moved, ((0, 0), (0, 0), (0, 0), (2 * g, rows_n + 2 - taps_r - 2 * g), (0, 0))
        ).reshape(c2, -1)
        for g in range(rows_n // 2)
    ]
    return jnp.concatenate(bands, axis=0)


def on_device(
    ref_features,
    source_tiles,
    pair_lists,
    view_counts,
    disparities,
    conv_first,
    bias_first,
    conv_second,
    bias_second,
):
    n_view = lax.axis_size("view")
    rows_n, channels, n_cols = ref_features.shape
    tiles_dev = source_tiles.shape[0]
    _, sources, blocks = pair_lists.shape
    planes = disparities.shape[0]
    c1 = conv_first.shape[2]
    c2 = conv_second.shape[0]
    request_total = sources * blocks
    slot_cap = max(2, (request_total + n_view - 1) // n_view)
    flat_ids = pair_lists.reshape(request_total)
    slot_ids, local_ids = request_slots(flat_ids, slot_cap, tiles_dev)
    wanted = request_table(slot_ids, local_ids, n_view, slot_cap)
    asked = ask_owners(wanted)
    outgoing = source_tiles[jnp.maximum(asked, 0)]
    arrived = lax.all_to_all(outgoing, "view", split_axis=0, concat_axis=0, tiled=True)
    arrived = arrived.reshape(n_view * slot_cap, 2 * channels, n_cols)
    w2 = banded_second(conv_second, rows_n)
    part = (rows_n + 2) * c1
    half_x = n_cols // 2
    wide = -(-half_x // 128) * 128
    b1 = jnp.broadcast_to(bias_first[None, :, None], (rows_n + 2, c1, 1)).reshape(part, 1)
    b2 = jnp.broadcast_to(bias_second[None, :, None], (rows_n // 2, c2, 1)).reshape(-1, 1)
    w1, pick = prepare(conv_first, rows_n, n_cols, wide)
    ready = (arrived, w1, w2, b1, b2, pick)
    arrived, w1, w2, b1, b2, pick = lax.optimization_barrier(ready)
    slots = slot_ids.reshape(sources, blocks)
    ref_flat = ref_features.reshape(rows_n * channels, n_cols)
    warp = functools.partial(variance, slots=slots, disparities=disparities)
    warp = functools.partial(warp, view_counts=view_counts, arrived=arrived, ref_flat=ref_flat)
    low, top = warp(((rows_n - 2, rows_n - 1), (0,)))
    above = passed_along(low, "view", 1)
    below = passed_along(top, "view", -1)
    (mid,) = warp((tuple(range(1, rows_n - 2)),))
    smem = pl.BlockSpec(memory_space=pltpu.SMEM)
    vmem = pl.BlockSpec(memory_space=pltpu.VMEM)
    first_strip = (lax.axis_index("view") == 0).astype(jnp.int32).reshape(1)
    return pl.pallas_call(
        conv_kernel,
        out_shape=jax.ShapeDtypeStruct((planes // 2, rows_n // 2, c2, half_x), jnp.float32),
        in_specs=[smem] + [vmem] * 10,
        out_specs=vmem,
        scratch_shapes=[
            pltpu.VMEM((planes, 3 * part, n_cols), jnp.float32),
            pltpu.VMEM((planes + 1, 3 * part, wide), jnp.bfloat16),
        ],
        compiler_params=pltpu.CompilerParams(vmem_limit_bytes=24 << 20),
        name="convolutions",
    )(first_strip, above, top, mid, low, below, w1, b1, w2, b2, pick)


def solution(mesh):
    return jax.shard_map(
        on_device,
        mesh=mesh,
        in_specs=(
            P(("groups", "view"), None, None),
            P(("groups", "view"), None, None, None),
            P(("groups", "view"), None, None),
            P(("groups", "view")),
            P("groups", None),
            P(),
            P(),
            P(),
            P(),
        ),
        out_specs=P("groups", "view", None, None),
        check_vma=False,
    )
```

profile of v0, /device:TPU:17, one launch (start us, length us, event | category | flops | bytes accessed | tf_op | source)
XLA Modules:
  0.0 75.8 jit_solution(2551582473646662077)
XLA Ops:
  0.0 0.9 %reshape.176 = s32[16]{0:T(128)S(1)} reshape(s32[1,4,4]{2,1,0:T(4,128)} %param.11) | data formatting | bytes 128 | tf_op jit(solution)/shard_map/reshape | solution.py:314
  0.9 0.2 convert_reduce_fusion
  1.1 0.1 select_reduce_fusion
  1.2 0.1 sub.15
  1.3 7.3 %ask.1 = s32[16,8,128]{2,1,0:T(8,128)S(1)} custom-call(s32[16,8,128]{2,1,0:T(8,128)S(1)} %broadcast_in_dim.27.wanted_ref), custom_call_target="tpu_custom_call" | custom-call | tf_op jit(solution)/shard_map/ask/pallas_call | solution.py:86
  8.7 0.1 reshape.188
  8.8 1.9 %gather_fusion = bf16[32,2,32,384]{3,2,1,0:T(8,128)(2,1)} fusion(bf16[32,2,32,384]{3,2,1,0:T(8,128)(2,1)S(1)} %copy-done, s32[1024]{0:T(1024)S(1)} %pad_clamp_fusion), kind=kCustom, calls=%fused_computation | custom fusion | bytes 3145856 | tf_op jit(solution)/shard_map/gather | solution.py:318
  10.7 6.4 %all-to-all-start = ((bf16[16,2,2,32,384]{4,3,2,1,0:T(8,128)(2,1)}), bf16[16,2,2,32,384]{4,3,2,1,0:T(8,128)(2,1)S(1)}, u32[]{:S(2)}, u32[]{:S(2)}) async-start(bf16[16,2,2,32,384]{4,3,2,1,0:T(8,128)(2,1)} %bitcast.36), calls=%async_computation | async-start | bytes 3145728 | tf_op jit(solution)/shard_map/all_to_all | solution.py:319
  17.2 0.7 reduce_sum.21
  18.5 0.6 broadcast_in_dim.52
  19.3 0.6 broadcast_in_dim.29
  19.9 0.7 reshape.178
  20.6 1.8 %fusion.11 = (bf16[16,3,3,10,8]{0,4,3,2,1:T(8,128)(2,1)}, bf16[16,3,3,10,8]{0,4,3,2,1:T(8,128)(2,1)}, bf16[16,3,3,10,8]{0,4,3,2,1:T(8,128)(2,1)}, bf16[16,3,3,10,8]{0,4,3,2,1:T(8,128)(2,1)S(1)}) fusion(bf16[16,3,3,3,8]{0,4,3,2,1:T(8,128)(2,1)} %param.16), kind=kLoop, calls=%fused_computation.34 | loop fusion | bytes 99072 | tf_op jit(solution)/shard_map/jit(_pad)/pad | solution.py:286
  22.4 1.0 %copy.37 = bf16[16,720]{1,0:T(8,128)(2,1)S(1)} copy(bf16[16,720]{0,1:T(8,128)(2,1)} %bitcast.40) | data formatting | bytes 46080 | tf_op jit(solution)/shard_map/reshape | solution.py:288
  23.4 1.6 %copy.40 = bf16[16,720]{1,0:T(8,128)(2,1)} copy(bf16[16,720]{0,1:T(8,128)(2,1)} %bitcast.39) | data formatting | bytes 46080 | tf_op jit(solution)/shard_map/reshape | solution.py:288
  25.1 1.6 %copy.39 = bf16[16,720]{1,0:T(8,128)(2,1)} copy(bf16[16,720]{0,1:T(8,128)(2,1)} %bitcast.38) | data formatting | bytes 46080 | tf_op jit(solution)/shard_map/reshape | solution.py:288
  26.7 0.7 copy.38
  27.4 0.7 pad.25.conv_ref
  28.2 0.3 prepare.1
  28.4 0.8 %copy-done.2 = bf16[384,768]{1,0:T(8,128)(2,1)} copy-done((bf16[384,768]{1,0:T(8,128)(2,1)}, bf16[384,768]{1,0:T(8,128)(2,1)S(1)}, u32[]{:S(2)}) %copy-start.2) | copy-done | bytes 589848
  29.3 0.7 copy-done.4
  29.9 0.8 %pad_maximum_fusion.w2_ref = bf16[64,720]{1,0:T(8,128)(2,1)S(1)} fusion(bf16[16,720]{1,0:T(8,128)(2,1)} %copy.40, bf16[16,720]{1,0:T(8,128)(2,1)} %copy.39, bf16[16,720]{1,0:T(8,128)(2,1)} %copy.38, bf16[16,720]{1,0:T(8,128)(2,1)S(1)} %copy.37), kind=kLoop, calls=%fused_computation.1 | loop fusion | flops 368640 | bytes 184320 | tf_op jit(solution)/shard_map/concatenate | solution.py:291
  30.7 0.7 fusion.6.slot_ref
  31.4 21.6 %all-to-all-done = bf16[16,2,2,32,384]{4,3,2,1,0:T(8,128)(2,1)S(1)} async-done(((bf16[16,2,2,32,384]{4,3,2,1,0:T(8,128)(2,1)}), bf16[16,2,2,32,384]{4,3,2,1,0:T(8,128)(2,1)S(1)}, u32[]{:S(2)}, u32[]{:S(2)}) %all-to-all-start) | async-done | bytes 1572896 | tf_op jit(solution)/shard_map/all_to_all | solution.py:319
  53.0 3.5 %variance3.1 = (bf16[8,64,384]{2,1,0:T(8,128)(2,1)}, bf16[8,32,384]{2,1,0:T(8,128)(2,1)}) custom-call(s32[4,4]{1,0:T(4,128)S(1)} %fusion.6.slot_ref, s32[8,4]{1,0:T(8,128)S(1)} %copy.41.disp_ref, s32[1]{0:T(128)S(6)} %copy.51.count_ref, bf16[32,64,384]{2,1,0:T(8,128)(2,1)S(1)} %bitcast.32, bf16[256,384]{1,0:T(8,128)(2,1)S(1)} %bitcast.34), custom_call_target="tpu_custom_call" | custom-call | flops 11796480 | bytes 1179648 | tf_op jit(solution)/shard_map/variance3/pallas_call | solution.py:153
  56.5 2.2 %collective-permute-start = (bf16[8,64,384]{2,1,0:T(8,128)(2,1)}, bf16[8,64,384]{2,1,0:T(8,128)(2,1)}, u32[]{:S(2)}, u32[]{:S(2)}) collective-permute-start(bf16[8,64,384]{2,1,0:T(8,128)(2,1)} %get-tuple-element.18.low_ref), channel_id=1, source_target_pairs={{0,1},{1,2},{2,3},{3,4},{4,5},{5,6},{6,7},{7,8},{8,9},{9,10},{10,1... | collective-permute-start | bytes 1179656 | tf_op jit(solution)/shard_map/ppermute | solution.py:14
  58.8 2.6 %collective-permute-start.1 = (bf16[8,32,384]{2,1,0:T(8,128)(2,1)}, bf16[8,32,384]{2,1,0:T(8,128)(2,1)}, u32[]{:S(2)}, u32[]{:S(2)}) collective-permute-start(bf16[8,32,384]{2,1,0:T(8,128)(2,1)} %get-tuple-element.19.top_ref), channel_id=1, source_target_pairs={{1,0},{2,1},{3,2},{4,3},{5,4},{6,5},{7,6},{8,7},{9,8},{10,9},{11,1... | collective-permute-start | bytes 589832 | tf_op jit(solution)/shard_map/ppermute | solution.py:14
  61.4 0.1 copy.44.b2_ref
  61.5 0.1 copy.43.b1_ref
  61.6 3.7 %variance5.1.mid_ref = bf16[8,160,384]{2,1,0:T(8,128)(2,1)S(1)} custom-call(s32[4,4]{1,0:T(4,128)S(1)} %fusion.6.slot_ref, s32[8,4]{1,0:T(8,128)S(1)} %copy.41.disp_ref, s32[1]{0:T(128)S(6)} %copy.51.count_ref, bf16[32,64,384]{2,1,0:T(8,128)(2,1)S(1)} %bitcast.33, bf16[256,384]{1,0:T(8,128)(2,1)S(1)} %bitcast.35), custom_call_target="tpu_custom_call" | custom-call | flops 19660800 | bytes 1966080 | tf_op jit(solution)/shard_map/variance5/pallas_call | solution.py:153
  65.3 3.9 %collective-permute-done.1.below_ref = bf16[8,32,384]{2,1,0:T(8,128)(2,1)} collective-permute-done((bf16[8,32,384]{2,1,0:T(8,128)(2,1)}, bf16[8,32,384]{2,1,0:T(8,128)(2,1)}, u32[]{:S(2)}, u32[]{:S(2)}) %collective-permute-start.1) | collective-permute-done | bytes 196640 | tf_op jit(solution)/shard_map/ppermute | solution.py:14
  69.2 6.6 %convolutions.1 = f32[4,4,16,192]{3,2,1,0:T(8,128)} custom-call(s32[1]{0:T(128)} %bitcast.first_strip_ref, bf16[8,64,384]{2,1,0:T(8,128)(2,1)} %collective-permute-done.above_ref, bf16[8,32,384]{2,1,0:T(8,128)(2,1)} %get-tuple-element.19.top_ref, bf16[8,160,384]{2,1,0:T(8,128)(2,1)S(1)} %variance5.1.mid_ref, bf16[8,64,384]{2,1,0:T(8,128)(2,1)} %get-tuple-element.18.low_ref, ...), custom_call_target="tpu_custom_call" | custom-call | tf_op jit(solution)/shard_map/convolutions/pallas_call | solution.py:341
  (35 shorter events, 0.2 us)
Async XLA Ops:
  0.0 8.8 %copy-start = (bf16[32,2,32,384]{3,2,1,0:T(8,128)(2,1)S(1)}, bf16[32,2,32,384]{3,2,1,0:T(8,128)(2,1)}, u32[]{:S(2)}) copy-start(bf16[32,2,32,384]{3,2,1,0:T(8,128)(2,1)} %param.10) | copy-start | bytes 4718596
  10.7 7.8 %copy-start.10 = (f32[16]{0:T(128)S(1)}, f32[16]{0:T(128)}, u32[]{:S(2)}) copy-start(f32[16]{0:T(128)} %param.17) | copy-start | bytes 196
  10.7 8.4 %copy-start.8 = (s32[8,4]{0,1:T(4,128)S(1)}, s32[8,4]{0,1:T(4,128)}, u32[]{:S(2)}) copy-start(s32[8,4]{0,1:T(4,128)} %param.13) | copy-start | bytes 388
  10.7 8.5 %copy-start.11 = (f32[8]{0:T(128)S(1)}, f32[8]{0:T(128)}, u32[]{:S(2)}) copy-start(f32[8]{0:T(128)} %param.15) | copy-start | bytes 100
  10.7 9.1 %copy-start.6 = (bf16[3,3,8,3,32]{4,2,3,1,0:T(8,128)(2,1)S(1)}, bf16[3,3,8,3,32]{4,2,3,1,0:T(8,128)(2,1)}, u32[]{:S(2)}) copy-start(bf16[3,3,8,3,32]{4,2,3,1,0:T(8,128)(2,1)} %param.14) | copy-start | bytes 41476
  10.7 42.2 %all-to-all-start = ((bf16[16,2,2,32,384]{4,3,2,1,0:T(8,128)(2,1)}), bf16[16,2,2,32,384]{4,3,2,1,0:T(8,128)(2,1)S(1)}, u32[]{:S(2)}, u32[]{:S(2)}) async-start(bf16[16,2,2,32,384]{4,3,2,1,0:T(8,128)(2,1)} %bitcast.36), calls=%async_computation | async-start | bytes 3145728 | tf_op jit(solution)/shard_map/all_to_all | solution.py:319
  17.2 35.8 %copy-start.1 = (bf16[8,32,384]{2,1,0:T(8,128)(2,1)S(1)}, bf16[8,32,384]{2,1,0:T(8,128)(2,1)}, u32[]{:S(2)}) copy-start(bf16[8,32,384]{2,1,0:T(8,128)(2,1)} %param.9) | copy-start | bytes 589828
  27.4 33.9 %copy-start.7 = (f32[64,1]{0,1:T(1,128)S(1)}, f32[64,1]{0,1:T(1,128)}, u32[]{:S(2)}) copy-start(f32[64,1]{0,1:T(1,128)} %broadcast_in_dim.52) | copy-start | bytes 772
  27.4 34.0 %copy-start.9 = (f32[80,1]{0,1:T(1,128)S(1)}, f32[80,1]{0,1:T(1,128)}, u32[]{:S(2)}) copy-start(f32[80,1]{0,1:T(1,128)} %broadcast_in_dim.29) | copy-start | bytes 964
  28.4 0.8 %copy-start.2 = (bf16[384,768]{1,0:T(8,128)(2,1)}, bf16[384,768]{1,0:T(8,128)(2,1)S(1)}, u32[]{:S(2)}) copy-start(bf16[384,768]{1,0:T(8,128)(2,1)S(1)} %get-tuple-element.24.pick_ref) | copy-start | bytes 1769476
  29.3 0.7 copy-start.4
  56.5 12.7 %collective-permute-start = (bf16[8,64,384]{2,1,0:T(8,128)(2,1)}, bf16[8,64,384]{2,1,0:T(8,128)(2,1)}, u32[]{:S(2)}, u32[]{:S(2)}) collective-permute-start(bf16[8,64,384]{2,1,0:T(8,128)(2,1)} %get-tuple-element.18.low_ref), channel_id=1, source_target_pairs={{0,1},{1,2},{2,3},{3,4},{4,5},{5,6},{6,7},{7,8},{8,9},{9,10},{10,1... | collective-permute-start | bytes 1179656 | tf_op jit(solution)/shard_map/ppermute | solution.py:14
  58.8 10.5 %collective-permute-start.1 = (bf16[8,32,384]{2,1,0:T(8,128)(2,1)}, bf16[8,32,384]{2,1,0:T(8,128)(2,1)}, u32[]{:S(2)}, u32[]{:S(2)}) collective-permute-start(bf16[8,32,384]{2,1,0:T(8,128)(2,1)} %get-tuple-element.19.top_ref), channel_id=1, source_target_pairs={{1,0},{2,1},{3,2},{4,3},{5,4},{6,5},{7,6},{8,7},{9,8},{10,9},{11,1... | collective-permute-start | bytes 589832 | tf_op jit(solution)/shard_map/ppermute | solution.py:14
  61.6 7.7 %copy-start.3 = (bf16[384,768]{1,0:T(8,128)(2,1)S(1)}, bf16[384,768]{1,0:T(8,128)(2,1)}, u32[]{:S(2)}) copy-start(bf16[384,768]{1,0:T(8,128)(2,1)} %copy-done.2) | copy-start | bytes 1769476
  61.6 7.7 %copy-start.5 = (bf16[360,224]{1,0:T(8,128)(2,1)S(1)}, bf16[360,224]{1,0:T(8,128)(2,1)}, u32[]{:S(2)}) copy-start(bf16[360,224]{1,0:T(8,128)(2,1)} %copy-done.4) | copy-start | bytes 483844
where the time goes:
time: 76.4 us; the launch traced here: 75.8 us
  waiting for transfers between devices  25.5 us (33%)
  Pallas kernels  21.5 us (28%)
  local copies, waits for them, and re-layouts  15 us (20%)
  starting transfers between devices  11.2 us (15%)
  other arithmetic  1.83 us (2%)
  between operations  0.83 us (1%)
    all_to_all x1, waiting for transfers between devices, on_device(): lax.all_to_all(outgoing, 'view', split_axis=0, concat_axis=0, tiled=True)  21.6 us
    pallas_call x1, Pallas kernels, ask_owners(): pl.pallas_call(functools.partial(ask_kernel, n_view), out_shape=jax.Shape...  7.35 us
    pallas_call x2, Pallas kernels, variance(): pl.pallas_call(functools.partial(variance_kernel, rows), out_shape=[jax.S...  7.26 us
    pallas_call x1, Pallas kernels, on_device(): pl.pallas_call(conv_kernel, out_shape=jax.ShapeDtypeStruct((planes // 2,...  6.61 us
    all_to_all x1, starting transfers between devices, on_device(): lax.all_to_all(outgoing, 'view', split_axis=0, concat_axis=0, tiled=True)  6.44 us
    reshape x4, local copies, waits for them, and re-layouts, banded_second(): bands = [jnp.pad(moved, ((0, 0), (0, 0), (0, 0), (2 * g, rows_n + 2 - tap...  5 us
    ppermute x2, starting transfers between devices, passed_along(): return lax.ppermute(x, axis, pairs)  4.79 us
    ppermute x2, waiting for transfers between devices, passed_along(): return lax.ppermute(x, axis, pairs)  3.93 us
  transfers between devices with their start and end apart: 3, of which 2 were waited for; matrix products, arithmetic and copies ran while one was open for 16% of the time, Pallas kernels for 5%

commit v1 on v0

v1 whole, which is shorter than its diff:
```python
import functools

import jax
import jax.numpy as jnp
from jax import lax
from jax.experimental import pallas as pl
from jax.experimental.pallas import tpu as pltpu
from jax.sharding import PartitionSpec as P

MESH = pl.DeviceIdType.MESH


def requests(pair_ref, tiles_dev):
    _, sources, blocks = pair_ref.shape
    ids = [pair_ref[0, s, b] for s in range(sources) for b in range(blocks)]
    owners = [jnp.where(i >= 0, i // tiles_dev, -1) for i in ids]
    locals_ = [i - o * tiles_dev for i, o in zip(ids, owners)]
    ranks = []
    for at, owner in enumerate(owners):
        rank = jnp.int32(0)
        for before in range(at):
            rank = rank + jnp.where(owners[before] == owner, 1, 0)
        ranks.append(rank)
    return owners, locals_, ranks


def exchange_kernel(
    n_view, slot_cap, pair_ref, count_ref, disp_ref, tiles_hbm, ref_hbm,
    var_ref,
    wanted_ref, asked_ref, asked_smem, tiles_ref, ref_ref, wide_ref, stage_ref, arrived_refs,
    local_sem, ref_sem, smem_sem, ask_send, ask_recv, data_send, data_recv, halo_send, halo_recv,
):
    me = lax.axis_index("view")
    barrier = pltpu.get_barrier_semaphore()

    def greet(step, carry):
        peer = lax.rem(me + step, n_view)
        pl.semaphore_signal(barrier, inc=1, device_id={"view": peer}, device_id_type=MESH)
        return carry

    lax.fori_loop(1, n_view, greet, 0)
    tiles_dev, tile_rows, channels, n_cols = tiles_ref.shape
    fetch = pltpu.make_async_copy(tiles_hbm, tiles_ref, local_sem)
    fetch.start()
    fetch_ref = pltpu.make_async_copy(ref_hbm, ref_ref, ref_sem)
    fetch_ref.start()

    sources, planes = disp_ref.shape[1], disp_ref.shape[0]
    blocks = pair_ref.shape[2]
    rows_n = blocks * tile_rows
    owners, locals_, ranks = requests(pair_ref, tiles_dev)
    shape = (n_view, 1, 128)
    row = lax.broadcasted_iota(jnp.int32, shape, 0)
    lane = lax.broadcasted_iota(jnp.int32, shape, 2)
    table = jnp.zeros(shape, jnp.int32)
    for owner, local, rank in zip(owners, locals_, ranks):
        table = jnp.where((row == owner) & (lane == rank), local, table)
    wanted_ref[...] = table
    slots = [jnp.maximum(o * slot_cap + r, 0) for o, r in zip(owners, ranks)]

    def peer_at(step):
        side = 1 - 2 * lax.rem(step, 2)
        return lax.rem(me + n_view // 2 + side * ((step + 1) // 2) + n_view, n_view)

    pl.semaphore_wait(barrier, n_view - 1)

    def ask_copy(peer, into):
        return pltpu.make_async_remote_copy(
            src_ref=wanted_ref.at[peer],
            dst_ref=asked_ref.at[into],
            send_sem=ask_send.at[peer],
            recv_sem=ask_recv.at[into],
            device_id={"view": peer},
            device_id_type=MESH,
        )

    def ask(step, carry):
        ask_copy(peer_at(step), me).start()
        return carry

    lax.fori_loop(0, n_view - 1, ask, 0)
    asked_ref[me] = wanted_ref[me]

    @pl.when(me == 0)
    def _():
        var_ref[:, 0 : 2 * channels] = jnp.zeros((planes, 2 * channels, n_cols), var_ref.dtype)

    @pl.when(me == n_view - 1)
    def _():
        var_ref[:, (rows_n + 2) * channels :] = jnp.zeros((planes, channels, n_cols), var_ref.dtype)

    def answered(step, carry):
        peer = peer_at(step)
        copy = ask_copy(peer, peer)
        copy.wait_send()
        copy.wait_recv()
        return carry

    lax.fori_loop(0, n_view - 1, answered, 0)
    to_smem = pltpu.make_async_copy(asked_ref, asked_smem, smem_sem)
    to_smem.start()
    fetch.wait()
    to_smem.wait()

    parts = stage_ref.shape[0]
    halves = parts // tile_rows
    depth = channels // halves

    def data_copy(part, peer, into):
        return pltpu.make_async_remote_copy(
            src_ref=stage_ref.at[part, peer],
            dst_ref=arrived_refs[part].at[into],
            send_sem=data_send.at[part, peer],
            recv_sem=data_recv.at[part, into],
            device_id={"view": peer},
            device_id_type=MESH,
        )

    for part in range(parts):
        of_row, half = part // halves, part % halves

        def gather(step, carry):
            peer = peer_at(step)
            for slot in range(slot_cap):
                index = asked_smem[peer, 0, slot]
                stage_ref[part, peer, slot] = tiles_ref[
                    index, of_row, half * depth : (half + 1) * depth
                ]
            return carry

        def send(step, carry):
            data_copy(part, peer_at(step), me).start()
            return carry

        lax.fori_loop(0, n_view - 1, gather, 0)
        lax.fori_loop(0, n_view - 1, send, 0)
    for part in range(parts):
        of_row, half = part // halves, part % halves
        for slot in range(slot_cap):
            index = asked_smem[me, 0, slot]
            arrived_refs[part][me, slot] = tiles_ref[
                index, of_row, half * depth : (half + 1) * depth
            ]

    fetch_ref.wait()
    live = count_ref[0]
    total = live.astype(jnp.float32) + 1.0
    inverse = 1.0 / jnp.full((1, n_cols), total, jnp.float32)
    column = lax.broadcasted_iota(jnp.int32, (depth, n_cols), 1)

    def halo_copy(row_at, half, out_row, peer, at):
        return pltpu.make_async_remote_copy(
            src_ref=var_ref.at[:, pl.ds((row_at + 2) * channels + half * depth, depth)],
            dst_ref=var_ref.at[:, pl.ds(out_row * channels + half * depth, depth)],
            send_sem=halo_send.at[at, half],
            recv_sem=halo_recv.at[at, half],
            device_id={"view": peer},
            device_id_type=MESH,
        )

    up = jnp.maximum(me - 1, 0)
    down = jnp.minimum(me + 1, n_view - 1)

    def upward(half):
        return halo_copy(0, half, rows_n + 2, up, 0)

    def downward(half, which):
        return halo_copy(rows_n - 2 + which, half, which, down, 1 + which)

    for part in range(parts):
        of_row, half = part // halves, part % halves

        def settle(step, carry):
            peer = peer_at(step)
            data_copy(part, peer, peer).wait_recv()
            return carry

        lax.fori_loop(0, n_view - 1, settle, 0)
        order = [block * tile_rows + of_row for block in range(blocks)]
        if of_row == tile_rows - 1:
            order = order[::-1]
        for source in range(sources):
            for place, row_at in enumerate(order):
                slot = slots[source * blocks + row_at // tile_rows]
                tile = arrived_refs[part][slot // slot_cap, slot % slot_cap].astype(jnp.float32)
                wide_ref[source, place] = jnp.where(source < live, tile, 0.0)

        def one_plane(plane, carry):
            offsets = [disp_ref[plane, source] for source in range(sources)]
            for place, row_at in enumerate(order):
                summed = ref_ref[row_at, half * depth : (half + 1) * depth].astype(jnp.float32)
                squares = summed * summed
                for source in range(sources):
                    offset = offsets[source]
                    turned = pltpu.roll(
                        wide_ref[source, place], jnp.where(offset < 0, offset + n_cols, offset), 1
                    )
                    origin = column - offset
                    inside = (origin >= 0) & (origin < n_cols)
                    turned = jnp.where(inside, turned, 0.0)
                    summed = summed + turned
                    squares = squares + turned * turned
                mean = summed * inverse
                at = (row_at + 2) * channels + half * depth
                var_ref[plane, at : at + depth] = (squares * inverse - mean * mean).astype(
                    jnp.bfloat16
                )
            return carry

        lax.fori_loop(0, planes, one_plane, 0)
        if of_row == 0:
            pl.when(me > 0)(lambda: upward(half).start())
        if of_row == tile_rows - 2:
            pl.when(me < n_view - 1)(lambda: downward(half, 0).start())
        if of_row == tile_rows - 1:
            pl.when(me < n_view - 1)(lambda: downward(half, 1).start())

    def sent(step, carry):
        for part in range(parts):
            peer = peer_at(step)
            data_copy(part, peer, peer).wait_send()
        return carry

    lax.fori_loop(0, n_view - 1, sent, 0)

    @pl.when(me > 0)
    def _():
        for half in range(halves):
            upward(half).wait_send()
            downward(half, 0).wait_recv()
            downward(half, 1).wait_recv()

    @pl.when(me < n_view - 1)
    def _():
        for half in range(halves):
            downward(half, 0).wait_send()
            downward(half, 1).wait_send()
            upward(half).wait_recv()


def exchange(pair_lists, view_counts, disparities, source_tiles, ref_features):
    n_view = lax.axis_size("view")
    rows_n, channels, n_cols = ref_features.shape
    tiles_dev, tile_rows = source_tiles.shape[:2]
    _, sources, blocks = pair_lists.shape
    planes = disparities.shape[0]
    slot_cap = max(2, (sources * blocks + n_view - 1) // n_view)
    halves = 2
    parts = tile_rows * halves
    depth = channels // halves
    hbm = pl.BlockSpec(memory_space=pltpu.HBM)
    smem = pl.BlockSpec(memory_space=pltpu.SMEM)
    vmem = pl.BlockSpec(memory_space=pltpu.VMEM)
    return pl.pallas_call(
        functools.partial(exchange_kernel, n_view, slot_cap),
        out_shape=jax.ShapeDtypeStruct((planes, (rows_n + 3) * channels, n_cols), jnp.bfloat16),
        in_specs=[smem, smem, smem, hbm, hbm],
        out_specs=vmem,
        scratch_shapes=[
            pltpu.VMEM((n_view, 1, 128), jnp.int32),
            pltpu.VMEM((n_view, 1, 128), jnp.int32),
            pltpu.SMEM((n_view, 1, 128), jnp.int32),
            pltpu.VMEM(source_tiles.shape, jnp.bfloat16),
            pltpu.VMEM(ref_features.shape, jnp.bfloat16),
            pltpu.VMEM((sources, blocks, depth, n_cols), jnp.float32),
            pltpu.VMEM((parts, n_view, slot_cap, depth, n_cols), jnp.bfloat16),
            [pltpu.VMEM((n_view, slot_cap, depth, n_cols), jnp.bfloat16)] * parts,
            pltpu.SemaphoreType.DMA,
            pltpu.SemaphoreType.DMA,
            pltpu.SemaphoreType.DMA,
            pltpu.SemaphoreType.DMA((n_view,)),
            pltpu.SemaphoreType.DMA((n_view,)),
            pltpu.SemaphoreType.DMA((parts, n_view)),
            pltpu.SemaphoreType.DMA((parts, n_view)),
            pltpu.SemaphoreType.DMA((3, halves)),
            pltpu.SemaphoreType.DMA((3, halves)),
        ],
        compiler_params=pltpu.CompilerParams(
            collective_id=0, has_side_effects=True, vmem_limit_bytes=24 << 20
        ),
        name="exchange",
    )(pair_lists, view_counts, disparities, source_tiles, ref_features)


def prepare_kernel(first_ref, second_ref, bias1_ref, bias2_ref, w1_ref, w2_ref, b1_ref, b2_ref, pick_ref):
    taps_p, taps_r, c1, taps_x, channels = first_ref.shape
    rows_out = w1_ref.shape[0] // (taps_p * taps_x * c1)
    width = w1_ref.shape[1]
    lanes = -(-width // 128) * 128
    for a in range(taps_p):
        slabs = [first_ref[a, b].astype(jnp.float32) for b in range(taps_r)]
        for d in range(taps_x):
            pieces = [slab[:, d, :] for slab in slabs]
            rest = jnp.zeros((c1, lanes - taps_r * channels), jnp.float32)
            base = jnp.concatenate(pieces + [rest], axis=1)
            for hi in range(rows_out):
                band = pltpu.roll(base, hi * channels, 1) if hi else base
                at = ((a * taps_x + d) * rows_out + hi) * c1
                w1_ref[at : at + c1] = band[:, :width].astype(jnp.bfloat16)
    c2 = second_ref.shape[0]
    half_r = w2_ref.shape[0] // c2
    part = b1_ref.shape[0]
    columns = w2_ref.shape[1]
    spread = []
    for a in range(taps_p):
        slabs = [second_ref[:, a, b].astype(jnp.float32) for b in range(taps_r)]
        for d in range(taps_x):
            spread += [slab[:, d, :] for slab in slabs]
            spread.append(jnp.zeros((c2, part - taps_r * c1), jnp.float32))
    wide2 = -(-columns // 128) * 128
    if wide2 > columns:
        spread.append(jnp.zeros((c2, wide2 - columns), jnp.float32))
    base = jnp.concatenate(spread, axis=1)
    for g in range(half_r):
        band = pltpu.roll(base, 2 * g * c1, 1) if g else base
        w2_ref[g * c2 : (g + 1) * c2] = band[:, :columns].astype(jnp.bfloat16)
    row = lax.rem(lax.broadcasted_iota(jnp.int32, b1_ref.shape, 0), c1)
    b1 = jnp.zeros(b1_ref.shape, jnp.float32)
    for o in range(c1):
        b1 = jnp.where(row == o, bias1_ref[o], b1)
    b1_ref[...] = b1
    row = lax.rem(lax.broadcasted_iota(jnp.int32, b2_ref.shape, 0), c2)
    b2 = jnp.zeros(b2_ref.shape, jnp.float32)
    for k in range(c2):
        b2 = jnp.where(row == k, bias2_ref[k], b2)
    b2_ref[...] = b2
    n_cols = pick_ref.shape[0]
    wide = pick_ref.shape[1] // 3
    source = lax.broadcasted_iota(jnp.int32, (n_cols, wide), 0)
    target = lax.broadcasted_iota(jnp.int32, (n_cols, wide), 1)
    for tap in range(3):
        hit = (source == 2 * target + (tap - 1)) & (target < n_cols // 2)
        pick_ref[:, tap * wide : (tap + 1) * wide] = jnp.where(hit, 1.0, 0.0).astype(jnp.bfloat16)


def prepare(conv_first, conv_second, bias_first, bias_second, rows_n, n_cols, wide):
    taps_p, taps_r, c1, taps_x, channels = conv_first.shape
    c2 = conv_second.shape[0]
    half_rows = (rows_n + 2) // 2
    part = (rows_n + 2) * c1
    vmem = pl.BlockSpec(memory_space=pltpu.VMEM)
    smem = pl.BlockSpec(memory_space=pltpu.SMEM)
    return pl.pallas_call(
        prepare_kernel,
        out_shape=[
            jax.ShapeDtypeStruct(
                (taps_p * taps_x * half_rows * c1, (half_rows + 2) * channels), jnp.bfloat16
            ),
            jax.ShapeDtypeStruct((rows_n // 2 * c2, taps_p * taps_x * part), jnp.bfloat16),
            jax.ShapeDtypeStruct((part, 128), jnp.float32),
            jax.ShapeDtypeStruct((rows_n // 2 * c2, 128), jnp.float32),
            jax.ShapeDtypeStruct((n_cols, 3 * wide), jnp.bfloat16),
        ],
        in_specs=[vmem, vmem, smem, smem],
        out_specs=[vmem] * 5,
        compiler_params=pltpu.CompilerParams(vmem_limit_bytes=8 << 20),
        name="prepare",
    )(conv_first, conv_second, bias_first, bias_second)


def conv_kernel(
    var_ref, w1_ref, b1_ref, w2_ref, b2_ref, pick_ref, out_ref, acc_ref, cost_ref,
):
    planes, _, n_cols = var_ref.shape
    half = w1_ref.shape[0] // 9
    part = 2 * half
    depth = w1_ref.shape[1]
    half_p, half_r, c2, half_x = out_ref.shape
    wide = pick_ref.shape[1] // 3
    weights = w1_ref[...]

    def one_plane(plane):
        block = var_ref[plane]
        skip = depth // (half_r + 3) * (half_r + 1)
        lower = block[skip:]
        products = (
            jnp.dot(weights, block[:depth], preferred_element_type=jnp.float32),
            jnp.dot(weights[:, : lower.shape[0]], lower, preferred_element_type=jnp.float32),
        )
        for tap in range(3):
            target = plane + 1 - tap
            if 0 <= target < planes:
                for shift in range(3):
                    for side in range(2):
                        start = (tap * 3 + shift) * half
                        piece = products[side][start : start + half]
                        at = slice(shift * part + side * half, shift * part + (side + 1) * half)
                        if tap == 0 or (tap == 1 and plane == 0):
                            acc_ref[target, at] = piece
                        else:
                            acc_ref[target, at] += piece

    column = lax.broadcasted_iota(jnp.int32, (part, n_cols), 1)
    row = lax.broadcasted_iota(jnp.int32, (part, n_cols), 0)
    hidden = (row < part // (2 * half_r + 2)) & (lax.axis_index("view") == 0)
    cost_ref[0] = jnp.zeros(cost_ref.shape[1:], cost_ref.dtype)
    bias1 = b1_ref[:, 0:1]
    bias2 = b2_ref[:, 0:1]

    def finish(plane):
        left = jnp.where(column == 0, 0.0, pltpu.roll(acc_ref[plane, 0:part], 1, 1))
        right = jnp.where(
            column == n_cols - 1, 0.0, pltpu.roll(acc_ref[plane, 2 * part : 3 * part], n_cols - 1, 1)
        )
        total = acc_ref[plane, part : 2 * part] + left + right + bias1
        cost = jnp.where(hidden, 0.0, jnp.maximum(total, 0.0)).astype(jnp.bfloat16)
        spread = jnp.dot(cost, pick_ref[...], preferred_element_type=jnp.float32)
        spread = spread.astype(jnp.bfloat16)
        for tap in range(3):
            cost_ref[plane + 1, tap * part : (tap + 1) * part] = spread[
                :, tap * wide : (tap + 1) * wide
            ]

    def second(q):
        block = cost_ref[2 * q : 2 * q + 3].reshape(9 * part, wide)
        result = jnp.dot(w2_ref[...], block, preferred_element_type=jnp.float32)
        result = result + bias2
        out_ref[q] = result[:, :half_x].reshape(half_r, c2, half_x)

    for plane in range(planes):
        one_plane(plane)
        if plane >= 1:
            finish(plane - 1)
            if plane % 2 == 0:
                second(plane // 2 - 1)
    finish(planes - 1)
    second(half_p - 1)


def on_device(
    ref_features,
    source_tiles,
    pair_lists,
    view_counts,
    disparities,
    conv_first,
    bias_first,
    conv_second,
    bias_second,
):
    rows_n, channels, n_cols = ref_features.shape
    planes = disparities.shape[0]
    c1 = conv_first.shape[2]
    c2 = conv_second.shape[0]
    part = (rows_n + 2) * c1
    half_x = n_cols // 2
    wide = -(-half_x // 128) * 128
    weights = prepare(conv_first, conv_second, bias_first, bias_second, rows_n, n_cols, wide)
    w1, w2, b1, b2, pick = weights
    volume = exchange(pair_lists, view_counts, disparities, source_tiles, ref_features)
    vmem = pl.BlockSpec(memory_space=pltpu.VMEM)
    return pl.pallas_call(
        conv_kernel,
        out_shape=jax.ShapeDtypeStruct((planes // 2, rows_n // 2, c2, half_x), jnp.float32),
        in_specs=[vmem] * 6,
        out_specs=vmem,
        scratch_shapes=[
            pltpu.VMEM((planes, 3 * part, n_cols), jnp.float32),
            pltpu.VMEM((planes + 1, 3 * part, wide), jnp.bfloat16),
        ],
        compiler_params=pltpu.CompilerParams(vmem_limit_bytes=24 << 20),
        name="convolutions",
    )(volume, w1, b1, w2, b2, pick)


def solution(mesh):
    return jax.shard_map(
        on_device,
        mesh=mesh,
        in_specs=(
            P(("groups", "view"), None, None),
            P(("groups", "view"), None, None, None),
            P(("groups", "view"), None, None),
            P(("groups", "view")),
            P("groups", None),
            P(),
            P(),
            P(),
            P(),
        ),
        out_specs=P("groups", "view", None, None),
        check_vma=False,
    )
```

time: 76.4 us -> 65.6 us (0.86)
  the two profiles are of different devices: /device:TPU:17 before, /device:TPU:18 now
where the time goes in v1:
time: 65.6 us; the launch traced here: 65.2 us
  Pallas kernels  57.7 us (88%)
  local copies, waits for them, and re-layouts  6.86 us (10%)
  between operations  0.7 us (1%)
    pallas_call x1, Pallas kernels, exchange(): pl.pallas_call(functools.partial(exchange_kernel, n_view, slot_cap), out_...  50.8 us
    unnamed x13, local copies, waits for them, and re-layouts  6.86 us
    pallas_call x1, Pallas kernels, on_device(): pl.pallas_call(conv_kernel, out_shape=jax.ShapeDtypeStruct((planes // 2,...  5.38 us
    pallas_call x1, Pallas kernels, prepare(): pl.pallas_call(prepare_kernel, out_shape=[jax.ShapeDtypeStruct((taps_p *...  1.54 us

profile of v1, /device:TPU:18, one launch (start us, length us, event | category | flops | bytes accessed | tf_op | source)
XLA Modules:
  0.0 65.2 jit_solution(3052954027094445821)
XLA Ops:
  0.7 0.8 %copy.10.disp_ref = s32[8,4]{1,0:T(8,128)S(1)} copy(s32[8,4]{0,1:T(4,128)} %param.13) | data formatting | bytes 256 | tf_op args[4]
  1.4 0.8 %copy.11.first_ref = bf16[3,3,8,3,32]{4,3,2,1,0:T(4,128)(2,1)S(1)} copy(bf16[3,3,8,3,32]{4,2,3,1,0:T(8,128)(2,1)} %param.14) | data formatting | bytes 27648 | tf_op args[5]
  2.3 0.9 %copy.12.second_ref = bf16[16,3,3,3,8]{4,3,2,1,0:T(4,128)(2,1)S(1)} copy(bf16[16,3,3,3,8]{0,4,3,2,1:T(8,128)(2,1)} %param.16) | data formatting | bytes 13824 | tf_op args[7]
  3.2 0.0 copy-start.3
  3.2 0.6 copy-done.3
  3.9 0.0 copy-start.4
  3.9 0.7 %copy-done.4 = f32[16]{0:T(128)S(1)} copy-done((f32[16]{0:T(128)S(1)}, f32[16]{0:T(128)}, u32[]{:S(2)}) %copy-start.4) | copy-done | bytes 88
  4.5 1.5 %prepare.1 = (bf16[360,224]{1,0:T(8,128)(2,1)S(1)}, bf16[64,720]{1,0:T(8,128)(2,1)S(1)}, f32[80,128]{1,0:T(8,128)S(1)}, f32[64,128]{1,0:T(8,128)S(1)}, bf16[384,768]{1,0:T(8,128)(2,1)S(1)}) custom-call(bf16[3,3,8,3,32]{4,3,2,1,0:T(4,128)(2,1)S(1)} %copy.11.first_ref, bf16[16,3,3,3,8]{4,3,2,1,0:T(4,128)(2,1)S(1)} %copy.12.second_ref, f32[8]{0:T(128)S(1)} %copy-done.3, ...), custom_call_target="tpu_custom_call" | custom-call | tf_op jit(solution)/shard_map/prepare/pallas_call | solution.py:343
  6.1 0.0 copy-start
  6.1 1.4 %copy-done = bf16[32,2,32,384]{3,2,1,0:T(8,128)(2,1)S(1)} copy-done((bf16[32,2,32,384]{3,2,1,0:T(8,128)(2,1)S(1)}, bf16[32,2,32,384]{3,2,1,0:T(8,128)(2,1)}, u32[]{:S(2)}) %copy-start) | copy-done | bytes 1572888
  7.5 0.0 copy-start.1
  7.5 0.9 %copy-done.1 = bf16[8,32,384]{2,1,0:T(8,128)(2,1)S(1)} copy-done((bf16[8,32,384]{2,1,0:T(8,128)(2,1)S(1)}, bf16[8,32,384]{2,1,0:T(8,128)(2,1)}, u32[]{:S(2)}) %copy-start.1) | copy-done | bytes 196632
  8.4 0.0 copy-start.2
  8.4 0.7 %copy-done.2 = s32[1,4,4]{2,1,0:T(4,128)S(1)} copy-done((s32[1,4,4]{2,1,0:T(4,128)S(1)}, s32[1,4,4]{2,1,0:T(4,128)}, u32[]{:S(2)}) %copy-start.2) | copy-done | bytes 88
  9.1 50.8 %exchange.1.var_ref = bf16[8,352,384]{2,1,0:T(8,128)(2,1)S(1)} custom-call(s32[1,4,4]{2,1,0:T(4,128)S(1)} %copy-done.2, s32[1]{0:T(128)S(6)} %copy.13.count_ref, s32[8,4]{1,0:T(8,128)S(1)} %copy.10.disp_ref, bf16[32,2,32,384]{3,2,1,0:T(8,128)(2,1)S(1)} %copy-done, bf16[8,32,384]{2,1,0:T(8,128)(2,1)S(1)} %copy-done.1), custom_call_target="tpu_custom_call" | custom-call | tf_op jit(solution)/shard_map/exchange/pallas_call | solution.py:254
  59.9 5.4 %convolutions.1 = f32[4,4,16,192]{3,2,1,0:T(8,128)} custom-call(bf16[8,352,384]{2,1,0:T(8,128)(2,1)S(1)} %exchange.1.var_ref, bf16[360,224]{1,0:T(8,128)(2,1)S(1)} %get-tuple-element.10.w1_ref, f32[80,128]{1,0:T(8,128)S(1)} %get-tuple-element.11.b1_ref, bf16[64,720]{1,0:T(8,128)(2,1)S(1)} %get-tuple-element.12.w2_ref, ...), custom_call_target="tpu_custom_call" | custom-call | tf_op jit(solution)/shard_map/convolutions/pallas_call | solution.py:452
Async XLA Ops:
  3.2 0.7 %copy-start.3 = (f32[8]{0:T(128)S(1)}, f32[8]{0:T(128)}, u32[]{:S(2)}) copy-start(f32[8]{0:T(128)} %bias1_ref.1) | copy-start | bytes 100
  3.9 0.7 %copy-start.4 = (f32[16]{0:T(128)S(1)}, f32[16]{0:T(128)}, u32[]{:S(2)}) copy-start(f32[16]{0:T(128)} %bias2_ref.1) | copy-start | bytes 196
  6.1 1.4 %copy-start = (bf16[32,2,32,384]{3,2,1,0:T(8,128)(2,1)S(1)}, bf16[32,2,32,384]{3,2,1,0:T(8,128)(2,1)}, u32[]{:S(2)}) copy-start(bf16[32,2,32,384]{3,2,1,0:T(8,128)(2,1)} %tiles_hbm.1) | copy-start | bytes 4718596
  7.5 0.9 %copy-start.1 = (bf16[8,32,384]{2,1,0:T(8,128)(2,1)S(1)}, bf16[8,32,384]{2,1,0:T(8,128)(2,1)}, u32[]{:S(2)}) copy-start(bf16[8,32,384]{2,1,0:T(8,128)(2,1)} %ref_hbm.1) | copy-start | bytes 589828
  8.4 0.7 %copy-start.2 = (s32[1,4,4]{2,1,0:T(4,128)S(1)}, s32[1,4,4]{2,1,0:T(4,128)}, u32[]{:S(2)}) copy-start(s32[1,4,4]{2,1,0:T(4,128)} %pair_ref.1) | copy-start | bytes 196

commit v2 on v1

v2 whole, which is shorter than its diff:
```python
import functools

import jax
import jax.numpy as jnp
from jax import lax
from jax.experimental import pallas as pl
from jax.experimental.pallas import tpu as pltpu
from jax.sharding import PartitionSpec as P

MESH = pl.DeviceIdType.MESH


def requests(pair_ref, tiles_dev):
    _, sources, blocks = pair_ref.shape
    ids = [pair_ref[0, s, b] for s in range(sources) for b in range(blocks)]
    owners = [jnp.where(i >= 0, i // tiles_dev, -1) for i in ids]
    locals_ = [i - o * tiles_dev for i, o in zip(ids, owners)]
    ranks = []
    for at, owner in enumerate(owners):
        rank = jnp.int32(0)
        for before in range(at):
            rank = rank + jnp.where(owners[before] == owner, 1, 0)
        ranks.append(rank)
    return owners, locals_, ranks


def prepare(first_ref, second_ref, bias1_ref, bias2_ref, own_refs, above_w, below_w, w2_ref, b1_ref, b2_ref, pick_ref):
    taps_p, taps_r, c1, taps_x, channels = first_ref.shape
    halves = len(own_refs) // 2
    depth = channels // halves
    rows_r = own_refs[0].shape[0] // (taps_x * c1)
    places = own_refs[0].shape[1] // (taps_p * depth)
    columns = taps_p * places * depth
    lanes = -(-columns // 128) * 128
    pieces = {}
    for a in range(taps_p):
        for b in range(taps_r):
            slab = first_ref[a, b].astype(jnp.float32)
            for d in range(taps_x):
                pieces[a, b, d] = slab[:, d, :]

    def zeros(rows, count):
        return jnp.zeros((rows, count), jnp.float32)

    for d in range(taps_x):
        for half in range(halves):
            cut = slice(half * depth, (half + 1) * depth)

            def base(taps):
                row = []
                for a in range(taps_p):
                    row += [zeros(c1, depth) if b is None else pieces[a, b, d][:, cut] for b in taps]
                    row.append(zeros(c1, (places - len(taps)) * depth))
                if lanes > columns:
                    row.append(zeros(c1, lanes - columns))
                return jnp.concatenate(row, axis=1)

            both, first, last, centre = base((0, 2)), base((0,)), base((2,)), base((1,))
            for parity in range(2):
                target = own_refs[parity * halves + half]
                for r in range(rows_r):
                    if (r - parity) % 2:
                        place = (r - 1 - parity) // 2
                        band = centre
                        inside = 0 <= place < places
                    else:
                        place = (r - 2 - parity) // 2
                        band = both
                        inside = True
                        if place < 0:
                            place, band, inside = place + 1, last, place + 1 == 0
                        elif place == places - 1:
                            band = first
                        elif place >= places:
                            inside = False
                    at = (d * rows_r + r) * c1
                    if not inside:
                        band = zeros(c1, columns)
                    elif place:
                        band = pltpu.roll(band, place * depth, 1)
                    target[at : at + c1] = band[:, :columns].astype(jnp.bfloat16)
        for r in range(2):
            row = []
            for a in range(taps_p):
                row += [pieces[a, 0, d], pieces[a, 1, d]] if r == 0 else [zeros(c1, channels), pieces[a, 0, d]]
            at = (d * 2 + r) * c1
            above_w[at : at + c1] = jnp.concatenate(row, axis=1).astype(jnp.bfloat16)
        row = [pieces[a, 2, d] for a in range(taps_p)]
        below_w[d * c1 : (d + 1) * c1] = jnp.concatenate(row, axis=1).astype(jnp.bfloat16)
    c2 = second_ref.shape[0]
    half_r = w2_ref.shape[0] // c2
    part = b1_ref.shape[0]
    columns = w2_ref.shape[1]
    spread = []
    for a in range(taps_p):
        slabs = [second_ref[:, a, b].astype(jnp.float32) for b in range(taps_r)]
        for d in range(taps_x):
            spread += [slab[:, d, :] for slab in slabs]
            spread.append(zeros(c2, part - taps_r * c1))
    wide2 = -(-columns // 128) * 128
    if wide2 > columns:
        spread.append(zeros(c2, wide2 - columns))
    base2 = jnp.concatenate(spread, axis=1)
    for g in range(half_r):
        band = pltpu.roll(base2, 2 * g * c1, 1) if g else base2
        w2_ref[g * c2 : (g + 1) * c2] = band[:, :columns].astype(jnp.bfloat16)
    row = lax.rem(lax.broadcasted_iota(jnp.int32, b1_ref.shape, 0), c1)
    b1 = jnp.zeros(b1_ref.shape, jnp.float32)
    for o in range(c1):
        b1 = jnp.where(row == o, bias1_ref[o], b1)
    b1_ref[...] = b1
    row = lax.rem(lax.broadcasted_iota(jnp.int32, b2_ref.shape, 0), c2)
    b2 = jnp.zeros(b2_ref.shape, jnp.float32)
    for k in range(c2):
        b2 = jnp.where(row == k, bias2_ref[k], b2)
    b2_ref[...] = b2
    n_cols = pick_ref.shape[0]
    wide = pick_ref.shape[1] // 3
    source = lax.broadcasted_iota(jnp.int32, (n_cols, wide), 0)
    target = lax.broadcasted_iota(jnp.int32, (n_cols, wide), 1)
    for tap in range(3):
        hit = (source == 2 * target + (tap - 1)) & (target < n_cols // 2)
        pick_ref[:, tap * wide : (tap + 1) * wide] = jnp.where(hit, 1.0, 0.0).astype(jnp.bfloat16)


def sweep_kernel(
    n_view, slot_cap, pair_ref, count_ref, disp_ref, bias1_ref, bias2_ref,
    tiles_hbm, ref_hbm, first_hbm, second_hbm,
    out_ref,
    wanted_ref, asked_ref, asked_smem, tiles_ref, ref_ref, first_ref, second_ref, wide_ref, stage_ref,
    arrived_refs, var_refs, above_ref, below_ref, own_refs, above_w, below_w, w2_ref, b1_ref, b2_ref,
    pick_ref, acc_ref, cost_ref,
    fetch_sem, smem_sem, ask_send, ask_recv, data_send, data_recv, halo_send, halo_recv,
):
    me = lax.axis_index("view")
    barrier = pltpu.get_barrier_semaphore()

    def greet(step, carry):
        peer = lax.rem(me + step, n_view)
        pl.semaphore_signal(barrier, inc=1, device_id={"view": peer}, device_id_type=MESH)
        return carry

    lax.fori_loop(1, n_view, greet, 0)
    tiles_dev, tile_rows, channels, n_cols = tiles_ref.shape
    pairs = ((tiles_hbm, tiles_ref), (ref_hbm, ref_ref), (first_hbm, first_ref), (second_hbm, second_ref))
    fetches = [
        pltpu.make_async_copy(src, dst, fetch_sem.at[at]) for at, (src, dst) in enumerate(pairs)
    ]
    for fetch in fetches:
        fetch.start()

    sources, planes = disp_ref.shape[1], disp_ref.shape[0]
    blocks = pair_ref.shape[2]
    owners, locals_, ranks = requests(pair_ref, tiles_dev)
    shape = (n_view, 1, 128)
    row = lax.broadcasted_iota(jnp.int32, shape, 0)
    lane = lax.broadcasted_iota(jnp.int32, shape, 2)
    table = jnp.zeros(shape, jnp.int32)
    for owner, local, rank in zip(owners, locals_, ranks):
        table = jnp.where((row == owner) & (lane == rank), local, table)
    wanted_ref[...] = table
    slots = [jnp.maximum(o * slot_cap + r, 0) for o, r in zip(owners, ranks)]

    def peer_at(step):
        side = 1 - 2 * lax.rem(step, 2)
        return lax.rem(me + n_view // 2 + side * ((step + 1) // 2) + n_view, n_view)

    pl.semaphore_wait(barrier, n_view - 1)

    def ask_copy(peer, into):
        return pltpu.make_async_remote_copy(
            src_ref=wanted_ref.at[peer],
            dst_ref=asked_ref.at[into],
            send_sem=ask_send.at[peer],
            recv_sem=ask_recv.at[into],
            device_id={"view": peer},
            device_id_type=MESH,
        )

    def ask(step, carry):
        ask_copy(peer_at(step), me).start()
        return carry

    lax.fori_loop(0, n_view - 1, ask, 0)
    asked_ref[me] = wanted_ref[me]

    @pl.when(me == 0)
    def _():
        above_ref[...] = jnp.zeros(above_ref.shape, above_ref.dtype)

    @pl.when(me == n_view - 1)
    def _():
        below_ref[...] = jnp.zeros(below_ref.shape, below_ref.dtype)

    for ref in (*var_refs, above_ref, below_ref):
        edge = jnp.zeros(ref.shape[1:], ref.dtype)
        ref[0] = edge
        ref[planes + 1] = edge
    cost_ref[0] = jnp.zeros(cost_ref.shape[1:], cost_ref.dtype)

    def answered(step, carry):
        peer = peer_at(step)
        copy = ask_copy(peer, peer)
        copy.wait_send()
        copy.wait_recv()
        return carry

    lax.fori_loop(0, n_view - 1, answered, 0)
    to_smem = pltpu.make_async_copy(asked_ref, asked_smem, smem_sem)
    to_smem.start()
    fetches[0].wait()
    to_smem.wait()

    parts = stage_ref.shape[0]
    halves = parts // tile_rows
    depth = channels // halves

    def data_copy(part, peer, into):
        return pltpu.make_async_remote_copy(
            src_ref=stage_ref.at[part, peer],
            dst_ref=arrived_refs[part].at[into],
            send_sem=data_send.at[part, peer],
            recv_sem=data_recv.at[part, into],
            device_id={"view": peer},
            device_id_type=MESH,
        )

    for part in range(parts):
        of_row, half = part // halves, part % halves

        def gather(step, carry):
            peer = peer_at(step)
            for slot in range(slot_cap):
                index = asked_smem[peer, 0, slot]
                stage_ref[part, peer, slot] = tiles_ref[
                    index, of_row, half * depth : (half + 1) * depth
                ]
            return carry

        def send(step, carry):
            data_copy(part, peer_at(step), me).start()
            return carry

        lax.fori_loop(0, n_view - 1, gather, 0)
        lax.fori_loop(0, n_view - 1, send, 0)
    for part in range(parts):
        of_row, half = part // halves, part % halves
        for slot in range(slot_cap):
            index = asked_smem[me, 0, slot]
            arrived_refs[part][me, slot] = tiles_ref[
                index, of_row, half * depth : (half + 1) * depth
            ]
    for fetch in fetches[1:]:
        fetch.wait()
    prepare(
        first_ref, second_ref, bias1_ref, bias2_ref, own_refs, above_w, below_w, w2_ref, b1_ref,
        b2_ref, pick_ref,
    )

    live = count_ref[0]
    total = live.astype(jnp.float32) + 1.0
    inverse = 1.0 / jnp.full((1, n_cols), total, jnp.float32)
    column = lax.broadcasted_iota(jnp.int32, (depth, n_cols), 1)
    up = jnp.maximum(me - 1, 0)
    down = jnp.minimum(me + 1, n_view - 1)

    def halo_copy(src, dst, at, half, peer):
        return pltpu.make_async_remote_copy(
            src_ref=src,
            dst_ref=dst,
            send_sem=halo_send.at[at, half],
            recv_sem=halo_recv.at[at, half],
            device_id={"view": peer},
            device_id_type=MESH,
        )

    own_planes = pl.ds(1, planes)
    bottom = pl.ds((blocks - 1) * depth, depth)

    def upward(half):
        return halo_copy(
            var_refs[half].at[own_planes, pl.ds(0, depth)],
            below_ref.at[own_planes, pl.ds(half * depth, depth)],
            0, half, up,
        )

    def downward(of_row, half):
        return halo_copy(
            var_refs[of_row * halves + half].at[own_planes, bottom],
            above_ref.at[own_planes, pl.ds(of_row * channels + half * depth, depth)],
            1 + of_row, half, down,
        )

    taps_x = 3
    piece_rows = acc_ref.shape[1] // taps_x
    c1 = above_w.shape[0] // (2 * taps_x)

    for part in range(parts):
        of_row, half = part // halves, part % halves

        def settle(step, carry):
            peer = peer_at(step)
            data_copy(part, peer, peer).wait_recv()
            return carry

        lax.fori_loop(0, n_view - 1, settle, 0)
        for source in range(sources):
            for place in range(blocks):
                slot = slots[source * blocks + place]
                tile = arrived_refs[part][slot // slot_cap, slot % slot_cap].astype(jnp.float32)
                wide_ref[source, place] = jnp.where(source < live, tile, 0.0)

        def variance(places):
            def one_plane(plane, carry):
                offsets = [disp_ref[plane, source] for source in range(sources)]
                for place in places:
                    row_at = place * tile_rows + of_row
                    summed = ref_ref[row_at, half * depth : (half + 1) * depth].astype(jnp.float32)
                    squares = summed * summed
                    for source in range(sources):
                        offset = offsets[source]
                        turned = pltpu.roll(
                            wide_ref[source, place],
                            jnp.where(offset < 0, offset + n_cols, offset),
                            1,
                        )
                        origin = column - offset
                        inside = (origin >= 0) & (origin < n_cols)
                        turned = jnp.where(inside, turned, 0.0)
                        summed = summed + turned
                        squares = squares + turned * turned
                    mean = summed * inverse
                    var_refs[part][plane + 1, place * depth : (place + 1) * depth] = (
                        squares * inverse - mean * mean
                    ).astype(jnp.bfloat16)
                return carry

            lax.fori_loop(0, planes, one_plane, 0)

        variance((0, blocks - 1))
        if of_row == 0:
            pl.when(me > 0)(lambda: upward(half).start())
        pl.when(me < n_view - 1)(lambda: downward(of_row, half).start())
        variance(tuple(range(1, blocks - 1)))
        weights = own_refs[part][...]
        for plane in range(planes):
            block = var_refs[part][plane : plane + 3].reshape(-1, n_cols)
            product = jnp.dot(weights, block, preferred_element_type=jnp.float32)
            if part == 0:
                acc_ref[plane] = product
            else:
                acc_ref[plane] += product
        if part == halves:
            @pl.when(me < n_view - 1)
            def _():
                for side in range(halves):
                    upward(side).wait_recv()

            weights = below_w[...]
            for plane in range(planes):
                block = below_ref[plane : plane + 3].reshape(-1, n_cols)
                product = jnp.dot(weights, block, preferred_element_type=jnp.float32)
                for tap in range(taps_x):
                    at = tap * piece_rows + blocks * tile_rows * c1
                    acc_ref[plane, at : at + c1] += product[tap * c1 : (tap + 1) * c1]

    @pl.when(me > 0)
    def _():
        for half in range(halves):
            for of_row in range(tile_rows):
                downward(of_row, half).wait_recv()

    half_p, half_r, c2, half_x = out_ref.shape
    wide = pick_ref.shape[1] // 3
    column = lax.broadcasted_iota(jnp.int32, (piece_rows, n_cols), 1)
    row = lax.broadcasted_iota(jnp.int32, (piece_rows, n_cols), 0)
    hidden = (row < c1) & (me == 0)
    bias1 = b1_ref[:, 0:1]
    bias2 = b2_ref[:, 0:1]

    def finish(plane):
        block = above_ref[plane : plane + 3].reshape(-1, n_cols)
        product = jnp.dot(above_w[...], block, preferred_element_type=jnp.float32)
        for tap in range(taps_x):
            at = tap * piece_rows
            acc_ref[plane, at : at + 2 * c1] += product[tap * 2 * c1 : (tap + 1) * 2 * c1]
        left = jnp.where(column == 0, 0.0, pltpu.roll(acc_ref[plane, 0:piece_rows], 1, 1))
        right = jnp.where(
            column == n_cols - 1,
            0.0,
            pltpu.roll(acc_ref[plane, 2 * piece_rows : 3 * piece_rows], n_cols - 1, 1),
        )
        total = acc_ref[plane, piece_rows : 2 * piece_rows] + left + right + bias1
        cost = jnp.where(hidden, 0.0, jnp.maximum(total, 0.0)).astype(jnp.bfloat16)
        spread = jnp.dot(cost, pick_ref[...], preferred_element_type=jnp.float32)
        spread = spread.astype(jnp.bfloat16)
        for tap in range(3):
            cost_ref[plane + 1, tap * piece_rows : (tap + 1) * piece_rows] = spread[
                :, tap * wide : (tap + 1) * wide
            ]

    def second(q):
        block = cost_ref[2 * q : 2 * q + 3].reshape(9 * piece_rows, wide)
        result = jnp.dot(w2_ref[...], block, preferred_element_type=jnp.float32)
        result = result + bias2
        out_ref[q] = result[:, :half_x].reshape(half_r, c2, half_x)

    for plane in range(planes):
        finish(plane)
        if plane % 2:
            second(plane // 2)

    def sent(step, carry):
        peer = peer_at(step)
        for part in range(parts):
            data_copy(part, peer, peer).wait_send()
        return carry

    lax.fori_loop(0, n_view - 1, sent, 0)

    @pl.when(me > 0)
    def _():
        for half in range(halves):
            upward(half).wait_send()

    @pl.when(me < n_view - 1)
    def _():
        for half in range(halves):
            for of_row in range(tile_rows):
                downward(of_row, half).wait_send()


def on_device(
    ref_features,
    source_tiles,
    pair_lists,
    view_counts,
    disparities,
    conv_first,
    bias_first,
    conv_second,
    bias_second,
):
    n_view = lax.axis_size("view")
    rows_n, channels, n_cols = ref_features.shape
    tiles_dev, tile_rows = source_tiles.shape[:2]
    _, sources, blocks = pair_lists.shape
    planes = disparities.shape[0]
    taps_p, _, c1, taps_x, _ = conv_first.shape
    c2 = conv_second.shape[0]
    slot_cap = max(2, (sources * blocks + n_view - 1) // n_view)
    halves = 2
    parts = tile_rows * halves
    depth = channels // halves
    part = (rows_n + 2) * c1
    half_x = n_cols // 2
    wide = -(-half_x // 128) * 128
    hbm = pl.BlockSpec(memory_space=pl.ANY)
    smem = pl.BlockSpec(memory_space=pltpu.SMEM)
    vmem = pl.BlockSpec(memory_space=pltpu.VMEM)
    bf16 = jnp.bfloat16
    return pl.pallas_call(
        functools.partial(sweep_kernel, n_view, slot_cap),
        out_shape=jax.ShapeDtypeStruct((planes // 2, rows_n // 2, c2, half_x), jnp.float32),
        in_specs=[smem] * 5 + [hbm] * 4,
        out_specs=vmem,
        scratch_shapes=[
            pltpu.VMEM((n_view, 1, 128), jnp.int32),
            pltpu.VMEM((n_view, 1, 128), jnp.int32),
            pltpu.SMEM((n_view, 1, 128), jnp.int32),
            pltpu.VMEM(source_tiles.shape, bf16),
            pltpu.VMEM(ref_features.shape, bf16),
            pltpu.VMEM(conv_first.shape, bf16),
            pltpu.VMEM(conv_second.shape, bf16),
            pltpu.VMEM((sources, blocks, depth, n_cols), jnp.float32),
            pltpu.VMEM((parts, n_view, slot_cap, depth, n_cols), bf16),
            [pltpu.VMEM((n_view, slot_cap, depth, n_cols), bf16)] * parts,
            [pltpu.VMEM((planes + 2, blocks * depth, n_cols), bf16)] * parts,
            pltpu.VMEM((planes + 2, 2 * channels, n_cols), bf16),
            pltpu.VMEM((planes + 2, channels, n_cols), bf16),
            [pltpu.VMEM((taps_x * part, taps_p * blocks * depth), bf16)] * parts,
            pltpu.VMEM((taps_x * 2 * c1, taps_p * 2 * channels), bf16),
            pltpu.VMEM((taps_x * c1, taps_p * channels), bf16),
            pltpu.VMEM((rows_n // 2 * c2, 9 * part), bf16),
            pltpu.VMEM((part, 128), jnp.float32),
            pltpu.VMEM((rows_n // 2 * c2, 128), jnp.float32),
            pltpu.VMEM((n_cols, 3 * wide), bf16),
            pltpu.VMEM((planes, taps_x * part, n_cols), jnp.float32),
            pltpu.VMEM((planes + 1, 3 * part, wide), bf16),
            pltpu.SemaphoreType.DMA((4,)),
            pltpu.SemaphoreType.DMA,
            pltpu.SemaphoreType.DMA((n_view,)),
            pltpu.SemaphoreType.DMA((n_view,)),
            pltpu.SemaphoreType.DMA((parts, n_view)),
            pltpu.SemaphoreType.DMA((parts, n_view)),
            pltpu.SemaphoreType.DMA((3, halves)),
            pltpu.SemaphoreType.DMA((3, halves)),
        ],
        compiler_params=pltpu.CompilerParams(
            collective_id=0, has_side_effects=True, vmem_limit_bytes=60 << 20
        ),
        name="sweep",
    )(
        pair_lists, view_counts, disparities, bias_first, bias_second,
        source_tiles, ref_features, conv_first, conv_second,
    )


def solution(mesh):
    return jax.shard_map(
        on_device,
        mesh=mesh,
        in_specs=(
            P(("groups", "view"), None, None),
            P(("groups", "view"), None, None, None),
            P(("groups", "view"), None, None),
            P(("groups", "view")),
            P("groups", None),
            P(),
            P(),
            P(),
            P(),
        ),
        out_specs=P("groups", "view", None, None),
        check_vma=False,
    )
```

time: 65.6 us -> 64.3 us (0.980)
  local copies, waits for them, and re-layouts: 6.86 us -> 6.08 us
    unnamed x13 -> x4, local copies, waits for them, and re-layouts: 6.86 us -> 6.08 us
    pallas_call x3 -> x1, Pallas kernels: 57.7 us -> 57.2 us  [on_device(): pl.pallas_call(functools.partial(sweep_kernel, n_view, slot_cap), out_sha...]
where the time goes in v2:
time: 64.3 us; the launch traced here: 64 us
  Pallas kernels  57.2 us (89%)
  local copies, waits for them, and re-layouts  6.08 us (9%)
  between operations  0.66 us (1%)
    pallas_call x1, Pallas kernels, on_device(): pl.pallas_call(functools.partial(sweep_kernel, n_view, slot_cap), out_sha...  57.2 us
    unnamed x4, local copies, waits for them, and re-layouts  6.08 us

profile of v2, /device:TPU:18, one launch (start us, length us, event | category | flops | bytes accessed | tf_op | source)
XLA Modules:
  0.0 64.0 jit_solution(5251018094039165101)
XLA Ops:
  0.7 1.3 %copy.10.disp_ref = s32[8,4]{1,0:T(8,128)} copy(s32[8,4]{0,1:T(4,128)} %param.13) | data formatting | bytes 256 | tf_op args[4]
  2.0 1.5 %copy.11.first_hbm = bf16[3,3,8,3,32]{4,3,2,1,0:T(4,128)(2,1)} copy(bf16[3,3,8,3,32]{4,2,3,1,0:T(8,128)(2,1)} %param.14) | data formatting | bytes 27648 | tf_op args[5]
  3.5 1.6 %copy.12.second_hbm = bf16[16,3,3,3,8]{4,3,2,1,0:T(4,128)(2,1)} copy(bf16[16,3,3,3,8]{0,4,3,2,1:T(8,128)(2,1)} %param.16) | data formatting | bytes 13824 | tf_op args[7]
  5.1 57.2 %sweep.1 = f32[4,4,16,192]{3,2,1,0:T(8,128)} custom-call(s32[1,4,4]{2,1,0:T(4,128)} %pair_ref.1, s32[1]{0:T(128)S(6)} %copy.14.count_ref, s32[8,4]{1,0:T(8,128)} %copy.10.disp_ref, f32[8]{0:T(128)} %bias1_ref.1, f32[16]{0:T(128)} %bias2_ref.1, bf16[32,2,32,384]{3,2,1,0:T(8,128)(2,1)} %tiles_hbm.1, bf16[8,32,384]{2,1,0:T(8,128)(2,1)} %ref_hbm.1, ...), custom_call_target="tpu_custom_call" | custom-call | tf_op jit(solution)/shard_map/sweep/pallas_call | solution.py:462
  62.3 1.7 %copy.15 = f32[4,4,16,192]{3,2,1,0:T(8,128)} copy(f32[4,4,16,192]{3,2,1,0:T(8,128)} %sweep.1) | data formatting | bytes 393216

commit v3 on v2

--- a/solution.py
+++ b/solution.py
@@ -24,8 +24,8 @@
     return owners, locals_, ranks
 
 
-def prepare(first_ref, second_ref, bias1_ref, bias2_ref, own_refs, above_w, below_w, w2_ref, b1_ref, b2_ref, pick_ref):
-    taps_p, taps_r, c1, taps_x, channels = first_ref.shape
+def prepare(first_ref, second_ref, bias1_ref, bias2_ref, own_refs, above_w, below_w, w2_ref, b1_ref, b2_ref, pick_ref, turn_ref):
+    taps_p, taps_r, taps_x, c1, channels = first_ref.shape
     halves = len(own_refs) // 2
     depth = channels // halves
     rows_r = own_refs[0].shape[0] // (taps_x * c1)
@@ -35,9 +35,8 @@
     pieces = {}
     for a in range(taps_p):
         for b in range(taps_r):
-            slab = first_ref[a, b].astype(jnp.float32)
             for d in range(taps_x):
-                pieces[a, b, d] = slab[:, d, :]
+                pieces[a, b, d] = first_ref[a, b, d].astype(jnp.float32)
 
     def zeros(rows, count):
         return jnp.zeros((rows, count), jnp.float32)
@@ -87,20 +86,17 @@
             above_w[at : at + c1] = jnp.concatenate(row, axis=1).astype(jnp.bfloat16)
         row = [pieces[a, 2, d] for a in range(taps_p)]
         below_w[d * c1 : (d + 1) * c1] = jnp.concatenate(row, axis=1).astype(jnp.bfloat16)
-    c2 = second_ref.shape[0]
+    c2 = second_ref.shape[-1]
     half_r = w2_ref.shape[0] // c2
     part = b1_ref.shape[0]
     columns = w2_ref.shape[1]
-    spread = []
+    turn_ref[...] = jnp.zeros(turn_ref.shape, jnp.float32)
     for a in range(taps_p):
-        slabs = [second_ref[:, a, b].astype(jnp.float32) for b in range(taps_r)]
         for d in range(taps_x):
-            spread += [slab[:, d, :] for slab in slabs]
-            spread.append(zeros(c2, part - taps_r * c1))
-    wide2 = -(-columns // 128) * 128
-    if wide2 > columns:
-        spread.append(zeros(c2, wide2 - columns))
-    base2 = jnp.concatenate(spread, axis=1)
+            for b in range(taps_r):
+                at = (a * taps_x + d) * part + b * c1
+                turn_ref[at : at + c1, 0:c2] = second_ref[a, b, d].astype(jnp.float32)
+    base2 = turn_ref[...].T[:c2]
     for g in range(half_r):
         band = pltpu.roll(base2, 2 * g * c1, 1) if g else base2
         w2_ref[g * c2 : (g + 1) * c2] = band[:, :columns].astype(jnp.bfloat16)
@@ -124,12 +120,12 @@
 
 
 def sweep_kernel(
-    n_view, slot_cap, pair_ref, count_ref, disp_ref, bias1_ref, bias2_ref,
+    n_view, slot_cap, pair_ref, count_ref, turned_disp_ref, bias1_ref, bias2_ref,
     tiles_hbm, ref_hbm, first_hbm, second_hbm,
     out_ref,
     wanted_ref, asked_ref, asked_smem, tiles_ref, ref_ref, first_ref, second_ref, wide_ref, stage_ref,
     arrived_refs, var_refs, above_ref, below_ref, own_refs, above_w, below_w, w2_ref, b1_ref, b2_ref,
-    pick_ref, acc_ref, cost_ref,
+    pick_ref, turn_ref, acc_ref, cost_ref,
     fetch_sem, smem_sem, ask_send, ask_recv, data_send, data_recv, halo_send, halo_recv,
 ):
     me = lax.axis_index("view")
@@ -149,7 +145,7 @@
     for fetch in fetches:
         fetch.start()
 
-    sources, planes = disp_ref.shape[1], disp_ref.shape[0]
+    sources, planes = turned_disp_ref.shape
     blocks = pair_ref.shape[2]
     owners, locals_, ranks = requests(pair_ref, tiles_dev)
     shape = (n_view, 1, 128)
@@ -254,7 +250,7 @@
         fetch.wait()
     prepare(
         first_ref, second_ref, bias1_ref, bias2_ref, own_refs, above_w, below_w, w2_ref, b1_ref,
-        b2_ref, pick_ref,
+        b2_ref, pick_ref, turn_ref,
     )
 
     live = count_ref[0]
@@ -312,7 +308,7 @@
 
         def variance(places):
             def one_plane(plane, carry):
-                offsets = [disp_ref[plane, source] for source in range(sources)]
+                offsets = [turned_disp_ref[source, plane] for source in range(sources)]
                 for place in places:
                     row_at = place * tile_rows + of_row
                     summed = ref_ref[row_at, half * depth : (half + 1) * depth].astype(jnp.float32)
@@ -448,6 +444,8 @@
     planes = disparities.shape[0]
     taps_p, _, c1, taps_x, _ = conv_first.shape
     c2 = conv_second.shape[0]
+    turned_first = jnp.transpose(conv_first, (0, 1, 3, 2, 4))
+    turned_second = jnp.transpose(conv_second, (1, 2, 3, 4, 0))
     slot_cap = max(2, (sources * blocks + n_view - 1) // n_view)
     halves = 2
     parts = tile_rows * halves
@@ -470,8 +468,8 @@
             pltpu.SMEM((n_view, 1, 128), jnp.int32),
             pltpu.VMEM(source_tiles.shape, bf16),
             pltpu.VMEM(ref_features.shape, bf16),
-            pltpu.VMEM(conv_first.shape, bf16),
-            pltpu.VMEM(conv_second.shape, bf16),
+            pltpu.VMEM(turned_first.shape, bf16),
+            pltpu.VMEM(turned_second.shape, bf16),
             pltpu.VMEM((sources, blocks, depth, n_cols), jnp.float32),
             pltpu.VMEM((parts, n_view, slot_cap, depth, n_cols), bf16),
             [pltpu.VMEM((n_view, slot_cap, depth, n_cols), bf16)] * parts,
@@ -485,6 +483,7 @@
             pltpu.VMEM((part, 128), jnp.float32),
             pltpu.VMEM((rows_n // 2 * c2, 128), jnp.float32),
             pltpu.VMEM((n_cols, 3 * wide), bf16),
+            pltpu.VMEM((-(-9 * part // 128) * 128, 128), jnp.float32),
             pltpu.VMEM((planes, taps_x * part, n_cols), jnp.float32),
             pltpu.VMEM((planes + 1, 3 * part, wide), bf16),
             pltpu.SemaphoreType.DMA((4,)),
@@ -501,8 +500,8 @@
         ),
         name="sweep",
     )(
-        pair_lists, view_counts, disparities, bias_first, bias_second,
-        source_tiles, ref_features, conv_first, conv_second,
+        pair_lists, view_counts, disparities.T, bias_first, bias_second,
+        source_tiles, ref_features, turned_first, turned_second,
     )
 
 

time: 64.3 us -> 59.7 us (0.928)
  local copies, waits for them, and re-layouts: 6.08 us -> 1.67 us
    unnamed x4 -> x1, local copies, waits for them, and re-layouts: 6.08 us -> 1.67 us
where the time goes in v3:
time: 59.7 us; the launch traced here: 59.6 us
  Pallas kernels  57.2 us (96%)
  local copies, waits for them, and re-layouts  1.67 us (3%)
  between operations  0.66 us (1%)
    pallas_call x1, Pallas kernels, on_device(): pl.pallas_call(functools.partial(sweep_kernel, n_view, slot_cap), out_sha...  57.2 us
    unnamed x1, local copies, waits for them, and re-layouts  1.67 us

profile of v3, /device:TPU:18, one launch (start us, length us, event | category | flops | bytes accessed | tf_op | source)
XLA Modules:
  0.0 59.6 jit_solution(16783199434068961786)
XLA Ops:
  0.7 57.2 %sweep.1 = f32[4,4,16,192]{3,2,1,0:T(8,128)} custom-call(s32[1,4,4]{2,1,0:T(4,128)} %pair_ref.1, s32[1]{0:T(128)S(6)} %copy.11.count_ref, s32[4,8]{1,0:T(4,128)} %bitcast.5, f32[8]{0:T(128)} %bias1_ref.1, f32[16]{0:T(128)} %bias2_ref.1, bf16[32,2,32,384]{3,2,1,0:T(8,128)(2,1)} %tiles_hbm.1, bf16[8,32,384]{2,1,0:T(8,128)(2,1)} %ref_hbm.1, ...), custom_call_target="tpu_custom_call" | custom-call | tf_op jit(solution)/shard_map/sweep/pallas_call | solution.py:460
  57.9 1.7 %copy.12 = f32[4,4,16,192]{3,2,1,0:T(8,128)} copy(f32[4,4,16,192]{3,2,1,0:T(8,128)} %sweep.1) | data formatting | bytes 393216
